TPU v7x, 128 devices: a whole 4x4x4 slice. The times are simulated.
128 devices in a mesh: row: 4 (over y), col: 32 (over x, z, core).
Axes of the slice: x: 4, y: 4, z: 4, core: 2. Of those that a mesh axis runs over, the one named last changes fastest.
Arguments:
- frontal: bfloat16 [16384, 49152], P('row', 'col')
- sample_cols: bfloat16 [49152, 64], P(('col', 'row')), may hold values from -6 to 6
- leaf_first: int32 [256], replicated, may hold values from 0 to 16352, as said below
- leaf_owner: int32 [256], replicated, may hold values from 0 to 31, as said below
- skeleton: int32 [256, 16], replicated, may hold values from 0 to 16383, as said below
Outputs:
- owner_samples: float32 [256, 8192], P('row', 'col')
- interp: float32 [64, 8192], P('row', 'col')
- worst: float32 [1], replicated
Inputs may be any that keep to these rules, and one draw needn't show every extreme that they name: `leaf_first`: leaves are consecutive and ascending; the first leaf of row group g starts at g * 4096; each row group has 64 leaves whose sizes are 1 to 5 times 32, in 16 runs of four consecutive leaves of together 256 rows. `leaf_owner`: each run of four leaves is owned by at most two devices of the group; the leaves one device owns in its group hold at most 256 rows and number at most 4; in every row group some device reaches both. Each leaf's skeleton rows are 16 distinct rows of that leaf, ascending.
All inputs are finite; a program needn't handle non-finite values.
Results may differ from a plain program's by a relative error of at most 0.0003.
Values may be sent and summed in bfloat16 or wider, within the bound.
A program may use at most 64 MiB of HBM per device.

v0:
```python
import jax
import jax.numpy as jnp
from jax import lax
from jax.sharding import PartitionSpec as P

LEAF_MOST = 4


def leaf_index(values, leaf_first):
    return jnp.sum((leaf_first[None, :] <= values[:, None]).astype(jnp.int32), axis=1) - 1


def local(frontal, sample_cols, leaf_first, leaf_owner, skeleton):
    highest = lax.Precision.HIGHEST
    group_rows, width = frontal.shape
    samples_count = sample_cols.shape[1]
    skel_count = skeleton.shape[1]
    leaves = leaf_first.shape[0]
    n_col = lax.axis_size("col")
    n_row = lax.axis_size("row")
    per_group = leaves // n_row
    total_rows = group_rows * n_row
    share_rows = group_rows // n_col
    capacity = 2 * share_rows
    row_pos = lax.axis_index("row")
    col_pos = lax.axis_index("col")
    rows = row_pos * group_rows + jnp.arange(group_rows, dtype=jnp.int32)
    row_leaf = leaf_index(rows, leaf_first)
    zero_entry = jnp.zeros((), frontal.dtype)
    piece = lax.all_gather(sample_cols, "row", axis=0, tiled=True)
    span = piece.shape[0]
    cols = col_pos * width + jnp.arange(span, dtype=jnp.int32)
    col_leaf = leaf_index(cols, leaf_first)
    same = (row_leaf[:, None] == col_leaf[None, :]) & (cols[None, :] < total_rows)
    kept = jnp.where(same, zero_entry, frontal)
    partial_value = jnp.dot(kept, piece, preferred_element_type=jnp.float32)
    ends = jnp.concatenate([leaf_first[1:], jnp.full((1,), total_rows, jnp.int32)])
    sizes = ends - leaf_first
    leaf_ids = jnp.arange(leaves, dtype=jnp.int32)
    group_of = leaf_ids // per_group
    own_hot = (leaf_owner[:, None] == jnp.arange(n_col, dtype=jnp.int32)[None, :]).astype(jnp.int32)
    weighted = (own_hot * sizes[:, None]).reshape(n_row, per_group, n_col)
    before = (jnp.cumsum(weighted, axis=1) - weighted).reshape(leaves, n_col)
    offset = jnp.sum(before * own_hot, axis=1)
    counted = own_hot.reshape(n_row, per_group, n_col)
    earlier = (jnp.cumsum(counted, axis=1) - counted).reshape(leaves, n_col)
    rank = jnp.sum(earlier * own_hot, axis=1)
    owned = (leaf_owner == col_pos) & (group_of == row_pos)
    slots = jnp.arange(capacity, dtype=jnp.int32)
    slot_hit = (
        owned[None, :]
        & (offset[None, :] <= slots[:, None])
        & (slots[:, None] < (offset + sizes)[None, :])
    )
    slot_hit_int = slot_hit.astype(jnp.int32)
    valid = jnp.any(slot_hit, axis=1)
    local_row = (
        jnp.sum(slot_hit_int * (leaf_first[None, :] + slots[:, None] - offset[None, :]), axis=1)
        - row_pos * group_rows
    )
    local_row = jnp.clip(local_row, 0, group_rows - 1)
    valid_float = valid[:, None].astype(jnp.float32)
    summed = lax.psum(partial_value, "col")
    mine = jnp.take(summed, local_row, axis=0) * valid_float
    select = owned[None, :] & (rank[None, :] == jnp.arange(LEAF_MOST, dtype=jnp.int32)[:, None])
    select_int = select.astype(jnp.int32)
    present = jnp.any(select, axis=1).astype(jnp.float32)
    skel_slot = jnp.sum(
        select_int[:, :, None] * (offset[:, None] + skeleton - leaf_first[:, None])[None, :, :],
        axis=1,
    )
    skel_slot = jnp.clip(skel_slot, 0, capacity - 1)
    picked = jnp.take(mine, skel_slot.reshape(-1), axis=0).reshape(
        LEAF_MOST, skel_count, samples_count
    )
    picked = picked * present[:, None, None]
    identity = jnp.eye(skel_count, dtype=jnp.float32)
    gram = jnp.einsum("kjp,kip->kji", picked, picked, precision=highest)
    gram = gram + (1.0 - present)[:, None, None] * identity[None, :, :]
    factor = jnp.linalg.cholesky(gram)
    inverse = jax.vmap(lambda lower: jax.scipy.linalg.cho_solve((lower, True), identity))(factor)
    slot_rank = jnp.sum(slot_hit_int * rank[None, :], axis=1)
    slot_pick = (
        (slot_rank[:, None] == jnp.arange(LEAF_MOST, dtype=jnp.int32)[None, :]) & valid[:, None]
    ).astype(jnp.float32)
    project = jnp.einsum("sp,kjp->skj", mine, picked, precision=highest)
    coeff_all = jnp.einsum("skj,kji->ski", project, inverse, precision=highest)
    coeff = jnp.sum(coeff_all * slot_pick[:, :, None], axis=1)
    rebuilt_all = jnp.einsum("ski,kip->skp", coeff_all, picked, precision=highest)
    rebuilt = jnp.sum(rebuilt_all * slot_pick[:, :, None], axis=1)
    resid = mine - rebuilt
    err = jnp.sum(slot_pick * jnp.sum(resid * resid, axis=1)[:, None], axis=0)
    norm = jnp.sum(slot_pick * jnp.sum(mine * mine, axis=1)[:, None], axis=0)
    ratio = jnp.sqrt(err) / jnp.sqrt(norm + 1e-06)
    local_worst = jnp.max(jnp.where(present > 0.5, ratio, 0.0)).reshape(1)
    worst = lax.pmax(local_worst, ("row", "col"))
    return (mine.T, coeff.T, worst)


def solution(mesh):
    return jax.shard_map(
        local,
        mesh=mesh,
        in_specs=(P("row", "col"), P(("col", "row"), None), P(), P(), P()),
        out_specs=(P("row", "col"), P("row", "col"), P()),
        check_vma=False,
    )
```

profile of v0, /device:TPU:0, one launch (start us, length us, event | category | flops | bytes accessed | tf_op | source)
XLA Modules:
  0.0 230.3 jit_solution(219416975980167111)
XLA Ops:
  7.2 13.1 %all_gather.3 = bf16[1536,64]{0,1:T(8,128)(2,1)S(1)} all-gather(bf16[384,64]{0,1:T(8,128)(2,1)} %param.6), channel_id=1, replica_groups=mesh['row'=4,'col'=32] {'row'}, dimensions={0}, use_global_device_ids=true | all-gather | bytes 245760 | tf_op jit(solution)/shard_map/all_gather | solution.py:30
  20.3 1.2 convert_reduce_fusion.1
  21.5 2.0 convert_reduce_fusion
  23.5 7.9 %fusion = f32[4096,64]{0,1:T(8,128)} fusion(bf16[1536,64]{0,1:T(8,128)(2,1)S(1)} %all_gather.3, bf16[4096,1536]{1,0:T(8,128)(2,1)} %param.5, s32[1536]{0:T(1024)S(1)} %broadcast_add_fusion.1, s32[4096]{0:T(1024)S(1)} %broadcast_add_fusion, pred[1536]{0:T(1024)(128)(4,1)S(1)} %broadcast_compare_fusion), kind=kOutput, calls=%fused_computation.3 | convolution fusion | flops 824180736 | bytes 13852160 | tf_op jit(solution)/shard_map/dot_general | solution.py:36
  32.3 0.3 select_reduce_fusion.2
  32.8 0.1 fusion.19
  32.9 0.2 select_reduce_fusion
  33.7 105.1 %all-reduce.2.cloned.1.call-done = f32[4096,64]{0,1:T(8,128)} async-done(((f32[4096,64]{0,1:T(8,128)}), f32[4096,64]{0,1:T(8,128)}) %all-reduce.2.cloned.1.call-update) | async-done | bytes 1048592 | tf_op jit(solution)/shard_map/psum | solution.py:63
  138.8 1.8 copy.23
  140.6 0.7 gather_fusion
  141.6 0.6 gather_fusion.1
  142.2 0.3 fusion.18
  142.5 0.3 fusion.8
  142.8 0.7 copy.28
  143.7 5.9 %custom-call.11 = f32[4,16,16]{2,1,0:T(8,128)S(1)} custom-call(f32[4,16,16]{2,1,0:T(8,128)S(1)} %fusion.17), custom_call_target="Cholesky" | custom-call | tf_op jit(solution)/shard_map/jit(cholesky)/cholesky | solution.py:80
  149.8 4.9 %custom-call.12 = f32[4,1,16,16]{2,3,1,0:T(8,128)S(1)} custom-call(f32[4,1,16,16]{3,2,1,0:T(8,128)S(1)} %select_bitcast_fusion), custom_call_target="InvertDiagBlocksLowerTriangular" | custom-call | tf_op jit(solution)/shard_map/vmap(jit(_cho_solve))/triangular_solve | solution.py:81
  154.7 0.3 fusion.14
  155.0 0.2 fusion.12
  155.2 0.8 multiply_reduce_fusion.2
  156.0 0.5 fusion.5
  156.6 0.3 multiply_reduce_fusion.1
  156.9 0.2 select_reduce_fusion.6
  157.1 0.6 fusion.36
  157.7 65.7 %pmax.7 = f32[1]{0:T(128)} all-reduce(f32[1]{0:T(128)} %bitcast.12), channel_id=1, replica_groups=mesh['row'=4,'col'=32] {'row','col'}, use_global_device_ids=true, to_apply=%region_21.22 | all-reduce | flops 1 | bytes 8 | tf_op jit(solution)/shard_map/pmax | solution.py:96
  (51 shorter events, 2.3 us)
Async XLA Ops:
  7.2 131.6 %all-reduce.2.cloned.1.call-start = ((), (), s32[]{:S(2)}) async-start(), calls=%async_computation | async-start | bytes 2097152 | tf_op jit(solution)/shard_map/psum | solution.py:63
  23.5 7.9 %copy-start = (s32[256]{0:T(256)S(1)}, s32[256]{0:T(256)}, u32[]{:S(2)}) copy-start(s32[256]{0:T(256)} %param.7) | copy-start | bytes 3076
  23.5 8.0 %copy-start.2 = (s32[256]{0:T(256)S(1)}, s32[256]{0:T(256)}, u32[]{:S(2)}) copy-start(s32[256]{0:T(256)} %param.8) | copy-start | bytes 3076
  23.5 9.9 %copy-start.1 = (s32[256,16]{0,1:T(8,128)S(1)}, s32[256,16]{0,1:T(8,128)}, u32[]{:S(2)}) copy-start(s32[256,16]{0,1:T(8,128)} %param.9) | copy-start | bytes 49156
Sparse Core Ops, SparseCore 0:
  31.5 107.2 all-reduce.1
where the time goes:
time: 231 us; the launch traced here: 230 us
  waiting for transfers between devices  105 us (45%)
  blocking collectives  78.8 us (34%)
  other arithmetic  17.2 us (7%)
  between operations  14.3 us (6%)
  matrix products  10.3 us (4%)
  local copies, waits for them, and re-layouts  4.54 us (2%)
    psum x1, waiting for transfers between devices, local(): summed = lax.psum(partial_value, 'col')  105 us
    pmax x1, blocking collectives, local(): worst = lax.pmax(local_worst, ('row', 'col'))  65.7 us
    all_gather x1, blocking collectives, local(): piece = lax.all_gather(sample_cols, 'row', axis=0, tiled=True)  13.1 us
    dot_general x1, matrix products, local(): partial_value = jnp.dot(kept, piece, preferred_element_type=jnp.float32)  7.88 us
    another operation x4, other arithmetic, local(): factor = jnp.linalg.cholesky(gram)  6.03 us
    another operation x3, other arithmetic, local(): jax.scipy.linalg.cho_solve((lower, True), identity)  5 us
  transfers between devices with their start and end apart: 1, of which 1 were waited for; matrix products, arithmetic and copies ran while one was open for 1% of the time, Pallas kernels for 0%

commit v1 on v0

v1 whole, which is shorter than its diff:
```python
import functools
import math

import jax
import jax.numpy as jnp
from jax import lax
from jax.experimental import pallas as pl
from jax.experimental.pallas import tpu as pltpu
from jax.sharding import PartitionSpec as P

UNIT = 32
RUN = 256
LANES = 128
LEAF_MOST = 4
F32 = jnp.float32
I32 = jnp.int32
MESH = pl.DeviceIdType.MESH
HI = lax.Precision.HIGHEST
NT = (((1,), (1,)), ((), ()))
NN = (((1,), (0,)), ((), ()))


def dot(a, b, dims, precision=None):
    return lax.dot_general(a, b, dims, precision=precision, preferred_element_type=F32)


def iota(shape, axis):
    return lax.broadcasted_iota(I32, shape, axis)


def kernel(
    cfg,
    frontal,
    piece,
    lf_s,
    lf_v,
    lo_v,
    sk_v,
    samples_out,
    interp_out,
    worst_out,
    a_v,
    pt,
    part,
    cx,
    s1,
    ph1,
    rot,
    pk,
    ph2,
    s3,
    mt,
    table_v,
    table_s,
    w0,
    w1,
    w2,
    w3,
    a_sem,
    t_sem,
    pc_send,
    pc_recv,
    cx_send,
    cx_recv,
    p1_send,
    p1_recv,
    p2_send,
    p2_recv,
    a2_send,
    a2_recv,
    m_send,
    m_recv,
):
    (rows, width, p_all, ny, nx, leaves_group, skel, cap, chunk) = cfg
    n_chunk = rows // chunk
    per_run = chunk // RUN
    tiles = rows // LANES
    half_p = p_all // 2
    sl = half_p // nx
    owners = 2 * nx
    per_owner = cap // UNIT
    depth = width // ny

    g = lax.axis_index("row")
    me = lax.axis_index("col")
    core = lax.rem(me, 2)
    z = lax.rem(me // 2, nx)
    x = me // (2 * nx)
    q = jnp.where(core == 0, x, z)
    b = jnp.where(core == 0, z, x)

    def col_of(xx, zz, cc):
        return (xx * nx + zz) * 2 + cc

    def ring_a(pos):
        return col_of(jnp.where(core == 0, pos, x), jnp.where(core == 0, z, pos), core)

    def ring_b(pos):
        return col_of(jnp.where(core == 0, x, pos), jnp.where(core == 0, pos, z), core)

    def remote(src, dst, send, recv, row, col):
        return pltpu.make_async_remote_copy(
            src_ref=src,
            dst_ref=dst,
            send_sem=send,
            recv_sem=recv,
            device_id=(row, col),
            device_id_type=MESH,
        )

    def load(i):
        at = pl.ds(pl.multiple_of(i * chunk, chunk), chunk)
        return pltpu.make_async_copy(frontal.at[at], a_v.at[at], a_sem.at[i])

    for i in range(n_chunk):
        load(i).start()

    barrier = pltpu.get_barrier_semaphore()
    count = 0
    for d in range(1, ny):
        pl.semaphore_signal(barrier, inc=1, device_id=(lax.rem(g + d, ny), me), device_id_type=MESH)
        count += 1
    j_x = x * 2 + core
    for d in range(1, owners):
        j = lax.rem(j_x + d, owners)
        to = col_of(j // 2, z, lax.rem(j, 2))
        pl.semaphore_signal(barrier, inc=1, device_id=(g, to), device_id_type=MESH)
        count += 1
    for d in range(1, nx):
        for cc in range(2):
            to = col_of(x, lax.rem(z + d, nx), cc)
            pl.semaphore_signal(barrier, inc=1, device_id=(g, to), device_id_type=MESH)
            count += 1
    pl.semaphore_wait(barrier, count)

    def piece_copy(d):
        at = pl.ds(pl.multiple_of(g * depth, LANES), depth)
        return remote(piece, pt.at[:, at], pc_send.at[d - 1], pc_recv.at[d - 1], lax.rem(g + d, ny), me)

    for d in range(1, ny):
        piece_copy(d).start()
    pt[:, pl.ds(pl.multiple_of(g * depth, LANES), depth)] = piece[...]

    nl = leaves_group
    lane = iota((1, LANES), 1)

    def group_lanes(v):
        out = None
        for gi in range(ny):
            part_v = v if gi == 0 else pltpu.roll(v, v.shape[1] - gi * nl, axis=1)
            part_v = part_v[:, :LANES]
            out = part_v if out is None else jnp.where(g == gi, part_v, out)
        return out

    first = group_lanes(lf_v[...])
    owner = group_lanes(lo_v[...])
    real = lane < nl
    owner = jnp.where(real, owner, -1)
    fu = jnp.where(real, (first - g * rows) // UNIT, 0)
    nxt = pltpu.roll(fu, LANES - 1, axis=1)
    nxt = jnp.where(lane == nl - 1, rows // UNIT, nxt)
    su = jnp.where(real, nxt - fu, 0)
    owner_t = jnp.transpose(jnp.broadcast_to(owner, (LANES, LANES)))
    fu_t = jnp.transpose(jnp.broadcast_to(fu, (LANES, LANES)))
    su_t = jnp.transpose(jnp.broadcast_to(su, (LANES, LANES)))
    li = iota((LANES, LANES), 0)
    lj = iota((LANES, LANES), 1)
    same = owner == owner_t
    before = same & (li < lj)
    after = same & (lj < li)
    off = jnp.sum(jnp.where(before, su_t, 0), axis=0, keepdims=True)
    rank = jnp.sum(jnp.where(before, 1, 0), axis=0, keepdims=True)
    off_t = jnp.sum(jnp.where(after, su, 0), axis=1, keepdims=True)
    rank_t = jnp.sum(jnp.where(after, 1, 0), axis=1, keepdims=True)
    slots_all = owners * nx * per_owner
    dst = iota((1, slots_all), 1)
    d_owner = dst // per_owner
    d_su = lax.rem(dst, per_owner)
    o1 = owner_t[:, :1]
    f1 = fu_t[:, :1]
    u1 = su_t[:, :1]
    hit = (o1 == d_owner) & (off_t <= d_su) & (d_su < off_t + u1)
    src = jnp.sum(jnp.where(hit, f1 + d_su - off_t + 1, 0), axis=0, keepdims=True) - 1
    per_tile = LANES // UNIT
    turn = lax.rem(d_su - src + 8 * per_tile * rows, per_tile)
    entry = jnp.where(src >= 0, turn * tiles + src // per_tile, per_tile * tiles)
    table_v[...] = entry
    to_smem = pltpu.make_async_copy(table_v, table_s, t_sem)
    to_smem.start()

    slot = iota((1, cap), 1)
    slot_u = slot // UNIT
    mine_t = (o1 == me) & (off_t <= slot_u) & (slot_u < off_t + u1)
    slot_rank = jnp.sum(jnp.where(mine_t, rank_t + 1, 0), axis=0, keepdims=True) - 1
    sk = group_lanes(sk_v[...])
    sk_slot = sk - first + off * UNIT + 1
    cols = []
    for k in range(LEAF_MOST):
        pick_k = (owner == me) & (rank == k)
        cols.append(jnp.sum(jnp.where(pick_k, sk_slot, 0), axis=1, keepdims=True))
    sk_col = jnp.concatenate(cols, axis=0)
    hot = jnp.where(sk_col == slot + 1, 1.0, 0.0).astype(F32)
    ki = LEAF_MOST * skel
    row_k = iota((ki, 1), 0) // skel

    for d in range(1, ny):
        piece_copy(d).wait_recv()

    def mask_run(t):
        run = g * (rows // RUN) + t
        blocks = width // RUN

        @pl.when(run // blocks == me)
        def _():
            r0 = pl.multiple_of(t * RUN, RUN)
            c0 = pl.multiple_of(lax.rem(run, blocks) * RUN, RUN)
            ri = iota((RUN, RUN), 0) + run * RUN
            ci = iota((RUN, RUN), 1) + run * RUN
            rl = jnp.zeros((RUN, RUN), I32)
            cl = jnp.zeros((RUN, RUN), I32)
            for k in range(1, 4):
                edge = lf_s[run * 4 + k]
                rl = rl + jnp.where(ri >= edge, 1, 0)
                cl = cl + jnp.where(ci >= edge, 1, 0)
            block = a_v[pl.ds(r0, RUN), pl.ds(c0, RUN)].astype(F32)
            a_v[pl.ds(r0, RUN), pl.ds(c0, RUN)] = jnp.where(rl == cl, 0.0, block).astype(jnp.bfloat16)

    sibling = col_of(x, z, 1 - core)

    def core_copy(i):
        at = pl.ds(pl.multiple_of(i * chunk, chunk), chunk)
        theirs = pl.ds(pl.multiple_of((1 - core) * half_p, half_p), half_p)
        return remote(part.at[theirs, at], cx.at[:, at], cx_send.at[i], cx_recv.at[i], g, sibling)

    def first_copy(i, d):
        to = lax.rem(q + d, nx)
        at = pl.ds(pl.multiple_of(i * chunk, chunk), chunk)
        rows_at = pl.ds(pl.multiple_of(to * sl, sl), sl)
        s = i * (nx - 1) + d - 1
        return remote(s1.at[rows_at, at], ph1.at[d - 1, :, at], p1_send.at[s], p1_recv.at[s], g, ring_a(to))

    def core_sum(i):
        at = pl.ds(pl.multiple_of(i * chunk, chunk), chunk)
        own = pl.ds(pl.multiple_of(core * half_p, half_p), half_p)
        core_copy(i).wait_recv()
        s1[:, at] = part[own, at] + cx[:, at]
        for d in range(1, nx):
            first_copy(i, d).start()

    def step(i, carry):
        load(i).wait()
        for t in range(per_run):
            mask_run(i * per_run + t)
        for t in range(per_run):
            at = pl.ds(pl.multiple_of(i * chunk + t * RUN, RUN), RUN)
            part[:, at] = dot(pt[...], a_v[at, :], NT)
        core_copy(i).start()

        @pl.when(i > 0)
        def _():
            core_sum(i - 1)

        return carry

    lax.fori_loop(0, n_chunk, step, 0)
    core_sum(n_chunk - 1)
    to_smem.wait()

    rot[per_tile * tiles] = jnp.zeros((sl, LANES), F32)

    def first_sum(i, carry):
        for d in range(1, nx):
            first_copy(i, d).wait_recv()
        own = pl.ds(pl.multiple_of(q * sl, sl), sl)
        for t in range(chunk // LANES):
            at = pl.ds(pl.multiple_of(i * chunk + t * LANES, LANES), LANES)
            v = s1[own, at]
            for d in range(1, nx):
                v = v + ph1[d - 1, :, at]
            tile = i * (chunk // LANES) + t
            rot[tile] = v
            for k in range(1, per_tile):
                rot[k * tiles + tile] = pltpu.roll(v, k * UNIT, axis=1)
        return carry

    lax.fori_loop(0, n_chunk, first_sum, 0)

    lane_u = iota((sl, LANES), 1) // UNIT

    def second_copy(d):
        to = lax.rem(b + d, nx)
        return remote(pk.at[d], ph2.at[d - 1], p2_send.at[d - 1], p2_recv.at[d - 1], g, ring_b(to))

    for d in [*range(1, nx), 0]:
        to = lax.rem(b + d, nx)

        def pack(j, carry, d=d, to=to):
            o = jnp.where(core == 0, col_of(j // 2, to, lax.rem(j, 2)), col_of(to, j // 2, lax.rem(j, 2)))
            for h in range(cap // LANES):
                base = o * per_owner + h * per_tile
                v = rot[table_s[0, base]]
                for k in range(1, per_tile):
                    v = jnp.where(lane_u == k, rot[table_s[0, base + k]], v)
                pk[d, :, pl.ds(pl.multiple_of(j * cap + h * LANES, LANES), LANES)] = v
            return carry

        lax.fori_loop(0, owners, pack, 0)
        if d > 0:
            second_copy(d).start()

    for d in range(1, nx):
        second_copy(d).wait_recv()
    total = pk[0]
    for d in range(1, nx):
        total = total + ph2[d - 1]
    s3[...] = total

    j_me = q * 2 + core
    slice_me = core * nx + q
    slice_rows = pl.ds(pl.multiple_of(slice_me * sl, sl), sl)

    def owner_copy(d):
        j = lax.rem(j_me + d, owners)
        to = jnp.where(core == 0, col_of(j // 2, z, lax.rem(j, 2)), col_of(x, j // 2, lax.rem(j, 2)))
        at = pl.ds(pl.multiple_of(j * cap, cap), cap)
        return remote(s3.at[:, at], mt.at[slice_rows, :], a2_send.at[d - 1], a2_recv.at[slice_me], g, to)

    def owner_wait(d):
        s = lax.rem(slice_me + d, owners)
        at = pl.ds(pl.multiple_of(s * sl, sl), sl)
        src_at = pl.ds(0, cap)
        return remote(s3.at[:, src_at], mt.at[at, :], a2_send.at[d - 1], a2_recv.at[s], g, sibling)

    for d in range(1, owners):
        owner_copy(d).start()
    mt[slice_rows, :] = s3[:, pl.ds(pl.multiple_of(j_me * cap, cap), cap)]
    for d in range(1, owners):
        owner_wait(d).wait_recv()

    m = mt[...]
    samples_out[...] = m
    pick = dot(hot, m, NT, HI)
    pick_t = dot(m, hot, NT, HI)
    rhs = dot(pick, m, NN, HI)
    gram = dot(pick, pick, NT, HI)
    col_k = iota((1, ki), 1) // skel
    in_block = row_k == col_k
    gram = jnp.where(in_block, gram, 0.0)
    folded = gram[:skel]
    for k in range(1, LEAF_MOST):
        folded = folded + gram[k * skel : (k + 1) * skel]
    here = jnp.concatenate(
        [jnp.broadcast_to(jnp.where(c[:1] > 0, 1, 0), (1, skel)) for c in cols], axis=1
    )
    eye_i = iota((skel, ki), 0)
    eye_r = lax.rem(iota((skel, ki), 1), skel)
    a = []
    for j in range(skel):
        v = None
        for k in range(LEAF_MOST):
            c = jnp.broadcast_to(folded[:, k * skel + j : k * skel + j + 1], (skel, ki))
            v = c if v is None else jnp.where(col_k == k, c, v)
        a.append(v + jnp.where((eye_i == j) & (here == 0), 1.0, 0.0))
    inv = jnp.where(eye_i == eye_r, 1.0, 0.0).astype(F32)
    for s in range(skel):
        col = a[s]
        rcp = 1.0 / col[s : s + 1]
        at_s = eye_i == s
        for j in range(s + 1, skel):
            t = a[j][s : s + 1] * rcp
            a[j] = jnp.where(at_s, t, a[j] - col * t)
        t = inv[s : s + 1] * rcp
        inv = jnp.where(at_s, t, inv - col * t)
    inv_all = jnp.where(in_block, jnp.concatenate([inv] * LEAF_MOST, axis=0), 0.0)
    rhs = jnp.where(row_k == slot_rank, rhs, 0.0)
    coeff = dot(inv_all, rhs, NN, HI)
    folded_c = coeff[:skel]
    for k in range(1, LEAF_MOST):
        folded_c = folded_c + coeff[k * skel : (k + 1) * skel]
    interp_out[...] = folded_c
    resid = m - dot(pick_t, coeff, NN, HI)
    err = jnp.sum(resid * resid, axis=0, keepdims=True)
    norm = jnp.sum(m * m, axis=0, keepdims=True)
    of_k = iota((8, 1), 0) == slot_rank
    err = jnp.sum(jnp.where(of_k, err, 0.0), axis=1, keepdims=True)
    norm = jnp.sum(jnp.where(of_k, norm, 0.0), axis=1, keepdims=True)
    ratio = jnp.sqrt(err) / jnp.sqrt(norm + 1e-06)
    w0[...] = jnp.broadcast_to(jnp.max(ratio, axis=0, keepdims=True), w0.shape)

    def m1(d):
        j = lax.rem(j_x + d, owners)
        return remote(w0, w1.at[d - 1], m_send.at[d - 1], m_recv.at[d - 1], g, col_of(j // 2, z, lax.rem(j, 2)))

    base2 = owners - 1
    base3 = base2 + nx - 1

    def m2(d):
        s = base2 + d - 1
        return remote(w2.at[0], w2.at[d], m_send.at[s], m_recv.at[s], g, col_of(x, lax.rem(z + d, nx), core))

    def m3(d):
        s = base3 + d - 1
        return remote(w3.at[0], w3.at[d], m_send.at[s], m_recv.at[s], lax.rem(g + d, ny), me)

    for d in range(1, owners):
        m1(d).start()
    for d in range(1, owners):
        m1(d).wait_recv()
    v = w0[...]
    for d in range(1, owners):
        v = jnp.maximum(v, w1[d - 1])
    w2[0] = v
    for d in range(1, nx):
        m2(d).start()
    for d in range(1, nx):
        m2(d).wait_recv()
    for d in range(1, nx):
        v = jnp.maximum(v, w2[d])
    w3[0] = v
    for d in range(1, ny):
        m3(d).start()
    for d in range(1, ny):
        m3(d).wait_recv()
    for d in range(1, ny):
        v = jnp.maximum(v, w3[d])
    worst_out[...] = v[:1]

    for d in range(1, ny):
        piece_copy(d).wait_send()
        m3(d).wait_send()

    def drain(i, carry):
        core_copy(i).wait_send()
        for d in range(1, nx):
            first_copy(i, d).wait_send()
        return carry

    lax.fori_loop(0, n_chunk, drain, 0)
    for d in range(1, nx):
        second_copy(d).wait_send()
        m2(d).wait_send()
    for d in range(1, owners):
        owner_copy(d).wait_send()
        m1(d).wait_send()


def local(frontal, sample_cols, leaf_first, leaf_owner, skeleton):
    rows, width = frontal.shape
    p_all = sample_cols.shape[1]
    leaves, skel = skeleton.shape
    ncol = lax.axis_size("col")
    ny = lax.axis_size("row")
    nx = math.isqrt(ncol // 2)
    cap = 2 * rows // ncol
    chunk = 512
    n_chunk = rows // chunk
    tiles = rows // LANES
    half_p = p_all // 2
    sl = half_p // nx
    owners = 2 * nx
    cfg = (rows, width, p_all, ny, nx, leaves // ny, skel, cap, chunk)
    slots_all = ncol * cap // UNIT
    vmem = pl.BlockSpec(memory_space=pltpu.VMEM)
    smem = pl.BlockSpec(memory_space=pltpu.SMEM)
    dma = pltpu.SemaphoreType.DMA
    n_m = owners - 1 + nx - 1 + ny - 1
    pad = ((0, 0), (0, max(0, LANES - leaves)))
    samples, interp, worst = pl.pallas_call(
        functools.partial(kernel, cfg),
        out_shape=(
            jax.ShapeDtypeStruct((p_all, cap), F32),
            jax.ShapeDtypeStruct((skel, cap), F32),
            jax.ShapeDtypeStruct((1, LANES), F32),
        ),
        in_specs=[pl.BlockSpec(memory_space=pl.ANY), vmem, smem, vmem, vmem, vmem],
        out_specs=(vmem, vmem, vmem),
        scratch_shapes=[
            pltpu.VMEM((rows, width), jnp.bfloat16),
            pltpu.VMEM((p_all, width), jnp.bfloat16),
            pltpu.VMEM((p_all, rows), F32),
            pltpu.VMEM((half_p, rows), F32),
            pltpu.VMEM((half_p, rows), F32),
            pltpu.VMEM((nx - 1, sl, rows), F32),
            pltpu.VMEM((4 * tiles + 1, sl, LANES), F32),
            pltpu.VMEM((nx, sl, owners * cap), F32),
            pltpu.VMEM((nx - 1, sl, owners * cap), F32),
            pltpu.VMEM((sl, owners * cap), F32),
            pltpu.VMEM((p_all, cap), F32),
            pltpu.VMEM((1, slots_all), I32),
            pltpu.SMEM((1, slots_all), I32),
            pltpu.VMEM((8, LANES), F32),
            pltpu.VMEM((owners - 1, 8, LANES), F32),
            pltpu.VMEM((nx, 8, LANES), F32),
            pltpu.VMEM((ny, 8, LANES), F32),
            dma((n_chunk,)),
            dma(()),
            dma((ny - 1,)),
            dma((ny - 1,)),
            dma((n_chunk,)),
            dma((n_chunk,)),
            dma((n_chunk * (nx - 1),)),
            dma((n_chunk * (nx - 1),)),
            dma((nx - 1,)),
            dma((nx - 1,)),
            dma((owners - 1,)),
            dma((owners,)),
            dma((n_m,)),
            dma((n_m,)),
        ],
        compiler_params=pltpu.CompilerParams(
            collective_id=0, has_side_effects=True, vmem_limit_bytes=60 << 20
        ),
        name="round",
    )(
        frontal,
        sample_cols.T,
        leaf_first,
        jnp.pad(leaf_first.reshape(1, leaves), pad),
        jnp.pad(leaf_owner.reshape(1, leaves), pad),
        jnp.pad(skeleton.T, pad),
    )
    return samples, interp, worst[0, :1]


def solution(mesh):
    return jax.shard_map(
        local,
        mesh=mesh,
        in_specs=(P("row", "col"), P(("col", "row"), None), P(), P(), P()),
        out_specs=(P("row", "col"), P("row", "col"), P()),
        check_vma=False,
    )
```

time: 231 us -> 50.7 us (0.22)
  waiting for transfers between devices: 105 us -> 0 us
  blocking collectives: 78.8 us -> 0 us
  Pallas kernels: 0 us -> 45.3 us
  other arithmetic: 17.2 us -> 0 us
  between operations: 14.3 us -> 2.33 us
  matrix products: 10.3 us -> 0 us
    psum x1 -> x0, waiting for transfers between devices: 105 us -> none  [local(): summed = lax.psum(partial_value, 'col')]
    pmax x1 -> x0, blocking collectives: 65.7 us -> none  [local(): worst = lax.pmax(local_worst, ('row', 'col'))]
    pallas_call x0 -> x1, Pallas kernels: none -> 45.3 us  [local(): pl.pallas_call(functools.partial(kernel, cfg), out_shape=(jax.ShapeDtypeS...]
    all_gather x1 -> x0, blocking collectives: 13.1 us -> none  [local(): piece = lax.all_gather(sample_cols, 'row', axis=0, tiled=True)]
    another operation x9 -> x0, other arithmetic: 11.3 us -> none  [the longest x4 6.03 us: local(): factor = jnp.linalg.cholesky(gram)]
    dot_general x5 -> x0, matrix products: 9.74 us -> none  [the longest x1 7.88 us: local(): partial_value = jnp.dot(kept, piece, preferred_element_type=jnp.float32)]
    reduce_sum x7 -> x0, other arithmetic: 4.27 us -> none  [the longest x2 3.14 us: leaf_index(): jnp.sum((leaf_first[None, :] <= values[:, None]).astype(jnp.int32), axis=1)]
  transfers between devices with their start and end apart: 1 -> 0, of which waited for: 1 -> 0; matrix products, arithmetic and copies ran while one was open for 1% -> 0% of each run, Pallas kernels for 0% -> 0%
where the time goes in v1:
time: 50.7 us; the launch traced here: 50.4 us
  Pallas kernels  45.3 us (89%)
  local copies, waits for them, and re-layouts  2.8 us (6%)
  between operations  2.33 us (5%)
    pallas_call x1, Pallas kernels, local(): pl.pallas_call(functools.partial(kernel, cfg), out_shape=(jax.ShapeDtypeS...  45.3 us
    unnamed x2, local copies, waits for them, and re-layouts  2.8 us

profile of v1, /device:TPU:0, one launch (start us, length us, event | category | flops | bytes accessed | tf_op | source)
XLA Modules:
  0.0 50.4 jit_solution(2128634433688722673)
XLA Ops:
  0.6 45.3 %round.1 = (f32[64,256]{1,0:T(8,128)}, f32[16,256]{1,0:T(8,128)}, f32[1,128]{1,0:T(1,128)}) custom-call(bf16[4096,1536]{1,0:T(8,128)(2,1)} %frontal.1, bf16[64,384]{1,0:T(8,128)(2,1)} %bitcast.6, s32[256]{0:T(256)} %lf_s.1, s32[1,256]{1,0:T(1,128)} %bitcast.8, s32[1,256]{1,0:T(1,128)} %bitcast.9, s32[16,256]{1,0:T(8,128)} %bitcast.7), custom_call_target="tpu_custom_call" | custom-call | tf_op jit(solution)/shard_map/round/pallas_call | solution.py:468
  45.9 1.5 %copy.11 = f32[64,256]{1,0:T(8,128)} copy(f32[64,256]{1,0:T(8,128)} %get-tuple-element.12) | data formatting | bytes 131072
  47.4 1.3 %copy.12 = f32[16,256]{1,0:T(8,128)} copy(f32[16,256]{1,0:T(8,128)} %get-tuple-element.13) | data formatting | bytes 32768

commit v2 on v1

v2 whole, which is shorter than its diff:
```python
import functools
import math

import jax
import jax.numpy as jnp
from jax import lax
from jax.experimental import pallas as pl
from jax.experimental.pallas import tpu as pltpu
from jax.sharding import PartitionSpec as P

UNIT = 32
RUN = 256
LANES = 128
LEAF_MOST = 4
F32 = jnp.float32
I32 = jnp.int32
MESH = pl.DeviceIdType.MESH
HI = lax.Precision.HIGHEST
NT = (((1,), (1,)), ((), ()))
NN = (((1,), (0,)), ((), ()))


def dot(a, b, dims, precision=None):
    return lax.dot_general(a, b, dims, precision=precision, preferred_element_type=F32)


def iota(shape, axis):
    return lax.broadcasted_iota(I32, shape, axis)


def out_kind(*shapes):
    return tuple(jax.ShapeDtypeStruct(s, F32) for s in shapes)


def kernel(
    cfg,
    frontal,
    piece,
    lf_h1,
    lf_h,
    lo_h,
    sk_h,
    samples_out,
    interp_out,
    worst_out,
    a_v,
    pt,
    lf_s,
    lf_v,
    lo_v,
    sk_v,
    part,
    cx,
    s1,
    ph1,
    rot,
    pk,
    rx,
    table_v,
    table_s,
    w0,
    w1,
    w2,
    w3,
    a_sem,
    l_sem,
    t_sem,
    near_sem,
    pc_send,
    pc_recv,
    cx_send,
    cx_recv,
    p1_send,
    p1_recv,
    o_send,
    o_recv,
    m_send,
    m_recv,
):
    (rows, width, p_all, ny, nx, leaves_group, skel, cap, chunk) = cfg
    n_chunk = rows // chunk
    per_run = chunk // RUN
    tiles = rows // LANES
    half_p = p_all // 2
    sl = half_p // nx
    owners = 2 * nx
    n_col = owners * nx
    per_owner = cap // UNIT
    depth = width // ny

    g = lax.axis_index("row")
    me = lax.axis_index("col")
    core = lax.rem(me, 2)
    z = lax.rem(me // 2, nx)
    x = me // (2 * nx)
    q = jnp.where(core == 0, x, z)
    j_x = x * 2 + core

    def col_of(xx, zz, cc):
        return (xx * nx + zz) * 2 + cc

    def ring_a(pos):
        return col_of(jnp.where(core == 0, pos, x), jnp.where(core == 0, z, pos), core)

    def remote(src, dst, send_at, recv_at, row, col):
        return pltpu.make_async_remote_copy(
            src_ref=src,
            dst_ref=dst,
            send_sem=send_at,
            recv_sem=recv_at,
            device_id=(row, col),
            device_id_type=MESH,
        )

    def signal(sem, row, col):
        pl.semaphore_signal(sem, inc=1, device_id=(row, col), device_id_type=MESH)

    barrier = pltpu.get_barrier_semaphore()
    count = 0
    for d in range(1, ny):
        signal(barrier, lax.rem(g + d, ny), me)
        count += 1
    for d in range(1, owners):
        j = lax.rem(j_x + d, owners)
        signal(barrier, g, col_of(j // 2, z, lax.rem(j, 2)))
        count += 1
    for d in range(1, nx):
        for cc in range(2):
            signal(barrier, g, col_of(x, lax.rem(z + d, nx), cc))
            count += 1

    def load(i):
        at = pl.ds(pl.multiple_of(i * chunk, chunk), chunk)
        return pltpu.make_async_copy(frontal.at[at], a_v.at[at], a_sem.at[i])

    own_at = pl.ds(pl.multiple_of(g * depth, LANES), depth)
    small = [
        pltpu.make_async_copy(piece, pt.at[:, own_at], l_sem.at[0]),
        pltpu.make_async_copy(lf_h1, lf_s, l_sem.at[1]),
        pltpu.make_async_copy(lf_h, lf_v, l_sem.at[2]),
        pltpu.make_async_copy(lo_h, lo_v, l_sem.at[3]),
        pltpu.make_async_copy(sk_h, sk_v, l_sem.at[4]),
    ]
    for c in small:
        c.start()
    for i in range(n_chunk):
        load(i).start()
    pl.semaphore_wait(barrier, count)

    drains = []

    def send(copy):
        copy().start()
        drains.append(lambda: copy().wait_send())

    def piece_copy(d):
        to = lax.rem(g + d, ny)
        return remote(piece, pt.at[:, own_at], pc_send.at[d - 1], pc_recv.at[d - 1], to, me)

    turns = sorted(range(1, ny), key=lambda d: min(d, ny - d))
    for d in turns:
        send(functools.partial(piece_copy, d))

    for d in range(1, nx):
        signal(near_sem, g, col_of(x, lax.rem(z + d, nx), core))
    for d in range(1, ny):
        signal(near_sem, lax.rem(g + d, ny), me)

    for c in small:
        c.wait()
    nl = leaves_group
    lane = iota((1, LANES), 1)

    def group_lanes(v):
        out = None
        for gi in range(ny):
            part_v = v if gi == 0 else pltpu.roll(v, v.shape[1] - gi * nl, axis=1)
            part_v = part_v[:, :LANES]
            out = part_v if out is None else jnp.where(g == gi, part_v, out)
        return out

    first = group_lanes(lf_v[...])
    owner = group_lanes(lo_v[...])
    real = lane < nl
    owner = jnp.where(real, owner, -1)
    fu = jnp.where(real, (first - g * rows) // UNIT, 0)
    nxt = pltpu.roll(fu, LANES - 1, axis=1)
    nxt = jnp.where(lane == nl - 1, rows // UNIT, nxt)
    su = jnp.where(real, nxt - fu, 0)
    owner_t = jnp.transpose(jnp.broadcast_to(owner, (LANES, LANES)))
    fu_t = jnp.transpose(jnp.broadcast_to(fu, (LANES, LANES)))
    su_t = jnp.transpose(jnp.broadcast_to(su, (LANES, LANES)))
    li = iota((LANES, LANES), 0)
    lj = iota((LANES, LANES), 1)
    same = owner == owner_t
    before = same & (li < lj)
    after = same & (lj < li)
    off = jnp.sum(jnp.where(before, su_t, 0), axis=0, keepdims=True)
    rank = jnp.sum(jnp.where(before, 1, 0), axis=0, keepdims=True)
    off_t = jnp.sum(jnp.where(after, su, 0), axis=1, keepdims=True)
    rank_t = jnp.sum(jnp.where(after, 1, 0), axis=1, keepdims=True)
    dst = iota((1, n_col * per_owner), 1)
    d_owner = dst // per_owner
    d_su = lax.rem(dst, per_owner)
    o1 = owner_t[:, :1]
    f1 = fu_t[:, :1]
    u1 = su_t[:, :1]
    hit = (o1 == d_owner) & (off_t <= d_su) & (d_su < off_t + u1)
    src = jnp.sum(jnp.where(hit, f1 + d_su - off_t + 1, 0), axis=0, keepdims=True) - 1
    per_tile = LANES // UNIT
    turn = lax.rem(d_su - src + 8 * per_tile * rows, per_tile)
    entry = jnp.where(src >= 0, turn * tiles + src // per_tile, per_tile * tiles)
    table_v[...] = entry
    to_smem = pltpu.make_async_copy(table_v, table_s, t_sem)
    to_smem.start()

    slot = iota((1, cap), 1)
    slot_u = slot // UNIT
    mine_t = (o1 == me) & (off_t <= slot_u) & (slot_u < off_t + u1)
    slot_rank = jnp.sum(jnp.where(mine_t, rank_t + 1, 0), axis=0, keepdims=True) - 1
    sk = group_lanes(sk_v[...])
    sk_slot = sk - first + off * UNIT + 1
    cols = []
    for k in range(LEAF_MOST):
        pick_k = (owner == me) & (rank == k)
        cols.append(jnp.sum(jnp.where(pick_k, sk_slot, 0), axis=1, keepdims=True))
    sk_col = jnp.concatenate(cols, axis=0)
    hot = jnp.where(sk_col == slot + 1, 1.0, 0.0).astype(F32)
    ki = LEAF_MOST * skel
    row_k = iota((ki, 1), 0) // skel

    def mask_run(t):
        run = g * (rows // RUN) + t
        blocks = width // RUN

        @pl.when(run // blocks == me)
        def _():
            r0 = pl.multiple_of(t * RUN, RUN)
            c0 = pl.multiple_of(lax.rem(run, blocks) * RUN, RUN)
            ri = iota((RUN, RUN), 0) + run * RUN
            ci = iota((RUN, RUN), 1) + run * RUN
            rl = jnp.zeros((RUN, RUN), I32)
            cl = jnp.zeros((RUN, RUN), I32)
            for k in range(1, 4):
                edge = lf_s[run * 4 + k]
                rl = rl + jnp.where(ri >= edge, 1, 0)
                cl = cl + jnp.where(ci >= edge, 1, 0)
            block = a_v[pl.ds(r0, RUN), pl.ds(c0, RUN)].astype(F32)
            a_v[pl.ds(r0, RUN), pl.ds(c0, RUN)] = jnp.where(rl == cl, 0.0, block).astype(jnp.bfloat16)

    def product(i, t, d):
        at = pl.ds(pl.multiple_of(i * chunk + t * RUN, RUN), RUN)
        k_at = pl.ds(pl.multiple_of(lax.rem(g + d, ny) * depth, LANES), depth)
        return at, dot(pt[:, k_at], a_v[at, k_at], NT)

    def own_step(i, carry):
        load(i).wait()
        for t in range(per_run):
            mask_run(i * per_run + t)
        for t in range(per_run):
            at, v = product(i, t, 0)
            part[:, at] = v
        return carry

    lax.fori_loop(0, n_chunk, own_step, 0)

    sibling = col_of(x, z, 1 - core)

    def core_copy(i):
        at = pl.ds(pl.multiple_of(i * chunk, chunk), chunk)
        theirs = pl.ds(pl.multiple_of((1 - core) * half_p, half_p), half_p)
        return remote(part.at[theirs, at], cx.at[:, at], cx_send.at[i], cx_recv.at[i], g, sibling)

    def add_step(i, carry, ds, last):
        for t in range(per_run):
            for d in ds:
                at, v = product(i, t, d)
                part[:, at] += v
        if last:
            core_copy(i).start()
        return carry

    for n, d in enumerate(turns):
        piece_copy(d).wait_recv()
        lax.fori_loop(0, n_chunk, functools.partial(add_step, ds=[ny - d], last=n == ny - 2), 0)

    def first_copy(i, d):
        to = lax.rem(q + d, nx)
        at = pl.ds(pl.multiple_of(i * chunk, chunk), chunk)
        rows_at = pl.ds(pl.multiple_of(to * sl, sl), sl)
        s = i * (nx - 1) + d - 1
        return remote(s1.at[rows_at, at], ph1.at[d - 1, :, at], p1_send.at[s], p1_recv.at[s], g, ring_a(to))

    def core_sum(i, carry):
        at = pl.ds(pl.multiple_of(i * chunk, chunk), chunk)
        own = pl.ds(pl.multiple_of(core * half_p, half_p), half_p)
        core_copy(i).wait_recv()
        s1[:, at] = part[own, at] + cx[:, at]
        for d in range(1, nx):
            first_copy(i, d).start()
        return carry

    def drain(i, carry):
        core_copy(i).wait_send()
        for d in range(1, nx):
            first_copy(i, d).wait_send()
        return carry

    lax.fori_loop(0, n_chunk, core_sum, 0)
    drains.append(lambda: lax.fori_loop(0, n_chunk, drain, 0))

    rot[per_tile * tiles] = jnp.zeros((sl, LANES), F32)

    def first_sum(i, carry):
        for d in range(1, nx):
            first_copy(i, d).wait_recv()
        own = pl.ds(pl.multiple_of(q * sl, sl), sl)
        for t in range(chunk // LANES):
            at = pl.ds(pl.multiple_of(i * chunk + t * LANES, LANES), LANES)
            v = s1[own, at]
            for d in range(1, nx):
                v = v + ph1[d - 1, :, at]
            tile = i * (chunk // LANES) + t
            rot[tile] = v
            for k in range(1, per_tile):
                rot[k * tiles + tile] = pltpu.roll(v, k * UNIT, axis=1)
        return carry

    lax.fori_loop(0, n_chunk, first_sum, 0)

    to_smem.wait()
    pl.semaphore_wait(near_sem, nx - 1 + ny - 1)
    lane_u = iota((sl, LANES), 1) // UNIT

    def owner_copy(k):
        to = lax.rem(me + k, n_col)
        return remote(pk.at[k], rx.at[me], o_send.at[k], o_recv.at[me], g, to)

    def owner_wait(k):
        frm = lax.rem(me + k, n_col)
        return remote(pk.at[k], rx.at[frm], o_send.at[k], o_recv.at[frm], g, frm)

    def block_of(o, h):
        base = o * per_owner + h * per_tile
        v = rot[table_s[0, base]]
        for k in range(1, per_tile):
            v = jnp.where(lane_u == k, rot[table_s[0, base + k]], v)
        return v

    def pack(k, carry):
        o = lax.rem(me + k, n_col)
        for h in range(cap // LANES):
            pk[k, :, h * LANES : (h + 1) * LANES] = block_of(o, h)
        owner_copy(k).start()
        return carry

    def owner_loop(do):
        def one(k, carry):
            do(k)
            return carry

        lax.fori_loop(1, n_col, one, 0)

    lax.fori_loop(1, n_col, pack, 0)
    for h in range(cap // LANES):
        rx[me, :, h * LANES : (h + 1) * LANES] = block_of(me, h)
    owner_loop(lambda k: owner_wait(k).wait_recv())
    drains.append(lambda: owner_loop(lambda k: owner_copy(k).wait_send()))

    def total(ids):
        v = rx[ids[0]]
        for s in ids[1:]:
            v = v + rx[s]
        return v

    m = jnp.concatenate(
        [total([col_of(a, b, 0) for b in range(nx)]) for a in range(nx)]
        + [total([col_of(b, a, 1) for b in range(nx)]) for a in range(nx)],
        axis=0,
    )

    samples_out[...] = m
    pick = dot(hot, m, NT, HI)
    pick_t = dot(m, hot, NT, HI)
    rhs = dot(pick, m, NN, HI)
    gram = dot(pick, pick, NT, HI)
    col_k = iota((1, ki), 1) // skel
    in_block = row_k == col_k
    gram = jnp.where(in_block, gram, 0.0)
    folded = gram[:skel]
    for k in range(1, LEAF_MOST):
        folded = folded + gram[k * skel : (k + 1) * skel]
    here = jnp.concatenate(
        [jnp.broadcast_to(jnp.where(c[:1] > 0, 1, 0), (1, skel)) for c in cols], axis=1
    )
    eye_i = iota((skel, ki), 0)
    eye_r = lax.rem(iota((skel, ki), 1), skel)
    a = []
    for j in range(skel):
        v = None
        for k in range(LEAF_MOST):
            c = jnp.broadcast_to(folded[:, k * skel + j : k * skel + j + 1], (skel, ki))
            v = c if v is None else jnp.where(col_k == k, c, v)
        a.append(v + jnp.where((eye_i == j) & (here == 0), 1.0, 0.0))
    inv = jnp.where(eye_i == eye_r, 1.0, 0.0).astype(F32)
    for s in range(skel):
        col = a[s]
        rcp = 1.0 / col[s : s + 1]
        at_s = eye_i == s
        for j in range(s + 1, skel):
            t = a[j][s : s + 1] * rcp
            a[j] = jnp.where(at_s, t, a[j] - col * t)
        t = inv[s : s + 1] * rcp
        inv = jnp.where(at_s, t, inv - col * t)
    inv_all = jnp.where(in_block, jnp.concatenate([inv] * LEAF_MOST, axis=0), 0.0)
    rhs = jnp.where(row_k == slot_rank, rhs, 0.0)
    coeff = dot(inv_all, rhs, NN, HI)
    resid = m - dot(pick_t, coeff, NN, HI)
    err = jnp.sum(resid * resid, axis=0, keepdims=True)
    norm = jnp.sum(m * m, axis=0, keepdims=True)
    of_k = iota((8, 1), 0) == slot_rank
    err = jnp.sum(jnp.where(of_k, err, 0.0), axis=1, keepdims=True)
    norm = jnp.sum(jnp.where(of_k, norm, 0.0), axis=1, keepdims=True)
    ratio = jnp.sqrt(err) / jnp.sqrt(norm + 1e-06)
    w0[...] = jnp.broadcast_to(jnp.max(ratio, axis=0, keepdims=True), w0.shape)

    def m1(d):
        j = lax.rem(j_x + d, owners)
        to = col_of(j // 2, z, lax.rem(j, 2))
        return remote(w0.at[:1], w1.at[d - 1, :1], m_send.at[d - 1], m_recv.at[d - 1], g, to)

    def m2(d):
        s = owners - 2 + d
        to_y = lax.rem(g + d // nx, ny)
        to = col_of(x, lax.rem(z + d % nx, nx), core)
        return remote(w2.at[:1], w3.at[d - 1, :1], m_send.at[s], m_recv.at[s], to_y, to)

    for d in range(1, owners):
        send(functools.partial(m1, d))
    folded_c = coeff[:skel]
    for k in range(1, LEAF_MOST):
        folded_c = folded_c + coeff[k * skel : (k + 1) * skel]
    interp_out[...] = folded_c
    for d in range(1, owners):
        m1(d).wait_recv()
    v = w0[:1]
    for d in range(1, owners):
        v = jnp.maximum(v, w1[d - 1, :1])
    w2[...] = jnp.broadcast_to(v, w2.shape)
    for d in range(1, nx * ny):
        send(functools.partial(m2, d))
    for f in drains:
        f()
    for d in range(1, nx * ny):
        m2(d).wait_recv()
    for d in range(1, nx * ny):
        v = jnp.maximum(v, w3[d - 1, :1])
    worst_out[...] = v


def finish(a_ref, b_ref, c_ref, a_out, b_out, c_out):
    a_out[...] = a_ref[...]
    b_out[...] = b_ref[...]
    c_out[...] = c_ref[:, :1]


def local(frontal, sample_cols, leaf_first, leaf_owner, skeleton):
    rows, width = frontal.shape
    p_all = sample_cols.shape[1]
    leaves, skel = skeleton.shape
    n_col = lax.axis_size("col")
    ny = lax.axis_size("row")
    nx = math.isqrt(n_col // 2)
    cap = 2 * rows // n_col
    chunk = 512
    n_chunk = rows // chunk
    tiles = rows // LANES
    half_p = p_all // 2
    sl = half_p // nx
    owners = 2 * nx
    cfg = (rows, width, p_all, ny, nx, leaves // ny, skel, cap, chunk)
    slots_all = n_col * cap // UNIT
    hbm = pl.BlockSpec(memory_space=pl.ANY)
    vmem = pl.BlockSpec(memory_space=pltpu.VMEM)
    dma = pltpu.SemaphoreType.DMA
    n_m = owners - 1 + nx * ny - 1
    pad = ((0, 0), (0, max(0, LANES - leaves)))
    wide = leaves + pad[1][1]
    results = pl.pallas_call(
        functools.partial(kernel, cfg),
        out_shape=out_kind((p_all, cap), (skel, cap), (1, LANES)),
        in_specs=[hbm] * 6,
        out_specs=(vmem, vmem, vmem),
        scratch_shapes=[
            pltpu.VMEM((rows, width), jnp.bfloat16),
            pltpu.VMEM((p_all, width), jnp.bfloat16),
            pltpu.SMEM((leaves,), I32),
            pltpu.VMEM((1, wide), I32),
            pltpu.VMEM((1, wide), I32),
            pltpu.VMEM((skel, wide), I32),
            pltpu.VMEM((p_all, rows), F32),
            pltpu.VMEM((half_p, rows), F32),
            pltpu.VMEM((half_p, rows), F32),
            pltpu.VMEM((nx - 1, sl, rows), F32),
            pltpu.VMEM((4 * tiles + 1, sl, LANES), F32),
            pltpu.VMEM((n_col, sl, cap), F32),
            pltpu.VMEM((n_col, sl, cap), F32),
            pltpu.VMEM((1, slots_all), I32),
            pltpu.SMEM((1, slots_all), I32),
            pltpu.VMEM((8, LANES), F32),
            pltpu.VMEM((owners - 1, 8, LANES), F32),
            pltpu.VMEM((8, LANES), F32),
            pltpu.VMEM((nx * ny - 1, 8, LANES), F32),
            dma((n_chunk,)),
            dma((5,)),
            dma(()),
            pltpu.SemaphoreType.REGULAR,
            dma((ny - 1,)),
            dma((ny - 1,)),
            dma((n_chunk,)),
            dma((n_chunk,)),
            dma((n_chunk * (nx - 1),)),
            dma((n_chunk * (nx - 1),)),
            dma((n_col,)),
            dma((n_col,)),
            dma((n_m,)),
            dma((n_m,)),
        ],
        compiler_params=pltpu.CompilerParams(
            collective_id=0, has_side_effects=True, vmem_limit_bytes=56 << 20
        ),
        name="round",
    )(
        frontal,
        sample_cols.T,
        leaf_first,
        jnp.pad(leaf_first.reshape(1, leaves), pad),
        jnp.pad(leaf_owner.reshape(1, leaves), pad),
        jnp.pad(skeleton.T, pad),
    )
    samples, interp, worst = pl.pallas_call(
        finish,
        out_shape=(
            jax.ShapeDtypeStruct((p_all, cap), F32),
            jax.ShapeDtypeStruct((skel, cap), F32),
            jax.ShapeDtypeStruct((1, 1), F32),
        ),
        in_specs=[vmem] * 3,
        out_specs=(vmem,) * 3,
        name="finish",
    )(*results)
    return samples, interp, worst.reshape(1)


def solution(mesh):
    return jax.shard_map(
        local,
        mesh=mesh,
        in_specs=(P("row", "col"), P(("col", "row"), None), P(), P(), P()),
        out_specs=(P("row", "col"), P("row", "col"), P()),
        check_vma=False,
    )
```

time: 50.7 us -> 44.1 us (0.87)
  local copies, waits for them, and re-layouts: 2.8 us -> 0 us
  Pallas kernels: 45.3 us -> 43.3 us
  between operations: 2.33 us -> 0.64 us
    unnamed x2 -> x0, local copies, waits for them, and re-layouts: 2.8 us -> none
    pallas_call x1 -> x2, Pallas kernels: 45.3 us -> 43.3 us  [the longest x1 41.9 us: local(): pl.pallas_call(functools.partial(kernel, cfg), out_shape=out_kind((p_all,...]
where the time goes in v2:
time: 44.1 us; the launch traced here: 44 us
  Pallas kernels  43.3 us (98%)
  between operations  0.64 us (1%)
    pallas_call x1, Pallas kernels, local(): pl.pallas_call(functools.partial(kernel, cfg), out_shape=out_kind((p_all,...  41.9 us
    pallas_call x1, Pallas kernels, local(): pl.pallas_call(finish, out_shape=(jax.ShapeDtypeStruct((p_all, cap), F32)...  1.5 us

profile of v2, /device:TPU:0, one launch (start us, length us, event | category | flops | bytes accessed | tf_op | source)
XLA Modules:
  0.0 44.0 jit_solution(18039367015092958536)
XLA Ops:
  0.6 41.9 %round.1 = (f32[64,256]{1,0:T(8,128)}, f32[16,256]{1,0:T(8,128)}, f32[1,128]{1,0:T(1,128)}) custom-call(bf16[4096,1536]{1,0:T(8,128)(2,1)} %frontal.1, bf16[64,384]{1,0:T(8,128)(2,1)} %bitcast.5, s32[256]{0:T(256)} %lf_h1.1, s32[1,256]{1,0:T(1,128)} %bitcast.7, s32[1,256]{1,0:T(1,128)} %bitcast.8, s32[16,256]{1,0:T(8,128)} %bitcast.6), custom_call_target="tpu_custom_call" | custom-call | tf_op jit(solution)/shard_map/round/pallas_call | solution.py:489
  42.5 1.5 %finish.1 = (f32[64,256]{1,0:T(8,128)}, f32[16,256]{1,0:T(8,128)}, f32[1,1]{1,0:T(1,128)}) custom-call(f32[64,256]{1,0:T(8,128)} %get-tuple-element.9.a_ref, f32[16,256]{1,0:T(8,128)} %get-tuple-element.10.b_ref, f32[1,128]{1,0:T(1,128)} %get-tuple-element.11.c_ref), custom_call_target="tpu_custom_call" | custom-call | tf_op jit(solution)/shard_map/finish/pallas_call | solution.py:541

commit v3 on v2

--- a/solution.py
+++ b/solution.py
@@ -29,7 +29,7 @@
 
 
 def out_kind(*shapes):
-    return tuple(jax.ShapeDtypeStruct(s, F32) for s in shapes)
+    return tuple(pltpu.VMEM(s, F32) for s in shapes)
 
 
 def kernel(
@@ -248,21 +248,16 @@
             block = a_v[pl.ds(r0, RUN), pl.ds(c0, RUN)].astype(F32)
             a_v[pl.ds(r0, RUN), pl.ds(c0, RUN)] = jnp.where(rl == cl, 0.0, block).astype(jnp.bfloat16)
 
-    def product(i, t, d):
-        at = pl.ds(pl.multiple_of(i * chunk + t * RUN, RUN), RUN)
+    def product(at, d):
         k_at = pl.ds(pl.multiple_of(lax.rem(g + d, ny) * depth, LANES), depth)
-        return at, dot(pt[:, k_at], a_v[at, k_at], NT)
-
-    def own_step(i, carry):
+        return dot(pt[:, k_at], a_v[at, k_at], NT)
+
+    for i in range(n_chunk):
         load(i).wait()
         for t in range(per_run):
             mask_run(i * per_run + t)
-        for t in range(per_run):
-            at, v = product(i, t, 0)
-            part[:, at] = v
-        return carry
-
-    lax.fori_loop(0, n_chunk, own_step, 0)
+        at = pl.ds(i * chunk, chunk)
+        part[:, at] = product(at, 0)
 
     sibling = col_of(x, z, 1 - core)
 
@@ -271,18 +266,14 @@
         theirs = pl.ds(pl.multiple_of((1 - core) * half_p, half_p), half_p)
         return remote(part.at[theirs, at], cx.at[:, at], cx_send.at[i], cx_recv.at[i], g, sibling)
 
-    def add_step(i, carry, ds, last):
-        for t in range(per_run):
-            for d in ds:
-                at, v = product(i, t, d)
-                part[:, at] += v
-        if last:
-            core_copy(i).start()
-        return carry
-
-    for n, d in enumerate(turns):
+    for d in turns[:-1]:
         piece_copy(d).wait_recv()
-        lax.fori_loop(0, n_chunk, functools.partial(add_step, ds=[ny - d], last=n == ny - 2), 0)
+        part[...] += product(pl.ds(0, rows), ny - d)
+    piece_copy(turns[-1]).wait_recv()
+    for i in range(n_chunk):
+        at = pl.ds(i * chunk, chunk)
+        part[:, at] += product(at, ny - turns[-1])
+        core_copy(i).start()
 
     def first_copy(i, d):
         to = lax.rem(q + d, nx)
@@ -332,13 +323,16 @@
     pl.semaphore_wait(near_sem, nx - 1 + ny - 1)
     lane_u = iota((sl, LANES), 1) // UNIT
 
-    def owner_copy(k):
-        to = lax.rem(me + k, n_col)
-        return remote(pk.at[k], rx.at[me], o_send.at[k], o_recv.at[me], g, to)
-
-    def owner_wait(k):
-        frm = lax.rem(me + k, n_col)
-        return remote(pk.at[k], rx.at[frm], o_send.at[k], o_recv.at[frm], g, frm)
+    def there(k):
+        dx, dz, dc = k
+        return col_of(lax.rem(x + dx, nx), lax.rem(z + dz, nx), lax.rem(core + dc, 2))
+
+    def owner_copy(n, k):
+        return remote(pk.at[n], rx.at[me], o_send.at[n], o_recv.at[me], g, there(k))
+
+    def owner_wait(n, k):
+        frm = there(k)
+        return remote(pk.at[n], rx.at[frm], o_send.at[n], o_recv.at[frm], g, frm)
 
     def block_of(o, h):
         base = o * per_owner + h * per_tile
@@ -347,25 +341,18 @@
             v = jnp.where(lane_u == k, rot[table_s[0, base + k]], v)
         return v
 
-    def pack(k, carry):
-        o = lax.rem(me + k, n_col)
+    steps = [(dx, dz, dc) for dx in range(nx) for dz in range(nx) for dc in range(2)]
+    steps.sort(key=lambda k: -(min(k[0], nx - k[0]) + min(k[1], nx - k[1])))
+    steps = [k for k in steps if k != (0, 0, 0)]
+    for n, k in enumerate(steps):
+        o = there(k)
         for h in range(cap // LANES):
-            pk[k, :, h * LANES : (h + 1) * LANES] = block_of(o, h)
-        owner_copy(k).start()
-        return carry
-
-    def owner_loop(do):
-        def one(k, carry):
-            do(k)
-            return carry
-
-        lax.fori_loop(1, n_col, one, 0)
-
-    lax.fori_loop(1, n_col, pack, 0)
+            pk[n, :, h * LANES : (h + 1) * LANES] = block_of(o, h)
+        send(functools.partial(owner_copy, n, k))
     for h in range(cap // LANES):
         rx[me, :, h * LANES : (h + 1) * LANES] = block_of(me, h)
-    owner_loop(lambda k: owner_wait(k).wait_recv())
-    drains.append(lambda: owner_loop(lambda k: owner_copy(k).wait_send()))
+    for n, k in reversed(list(enumerate(steps))):
+        owner_wait(n, k).wait_recv()
 
     def total(ids):
         v = rx[ids[0]]
@@ -503,7 +490,7 @@
             pltpu.VMEM((half_p, rows), F32),
             pltpu.VMEM((nx - 1, sl, rows), F32),
             pltpu.VMEM((4 * tiles + 1, sl, LANES), F32),
-            pltpu.VMEM((n_col, sl, cap), F32),
+            pltpu.VMEM((n_col - 1, sl, cap), F32),
             pltpu.VMEM((n_col, sl, cap), F32),
             pltpu.VMEM((1, slots_all), I32),
             pltpu.SMEM((1, slots_all), I32),
@@ -548,7 +535,7 @@
         in_specs=[vmem] * 3,
         out_specs=(vmem,) * 3,
         name="finish",
-    )(*results)
+    )(*(pltpu.with_memory_space_constraint(r, pltpu.VMEM) for r in results))
     return samples, interp, worst.reshape(1)
 
 

time: 44.1 us -> 38.8 us (0.88)
  Pallas kernels: 43.3 us -> 38.1 us
    pallas_call x1, Pallas kernels: 41.9 us -> 37.4 us  [local(): pl.pallas_call(functools.partial(kernel, cfg), out_shape=out_kind((p_all,...]
    pallas_call x1, Pallas kernels: 1.5 us -> 0.64 us  [local(): pl.pallas_call(finish, out_shape=(jax.ShapeDtypeStruct((p_all, cap), F32)...]
where the time goes in v3:
time: 38.8 us; the launch traced here: 38.7 us
  Pallas kernels  38.1 us (98%)
  between operations  0.64 us (2%)
    pallas_call x1, Pallas kernels, local(): pl.pallas_call(functools.partial(kernel, cfg), out_shape=out_kind((p_all,...  37.4 us

profile of v3, /device:TPU:0, one launch (start us, length us, event | category | flops | bytes accessed | tf_op | source)
XLA Modules:
  0.0 38.7 jit_solution(10509487976546537994)
XLA Ops:
  0.6 37.4 %round.1 = (f32[64,256]{1,0:T(8,128)S(1)}, f32[16,256]{1,0:T(8,128)S(1)}, f32[1,128]{1,0:T(1,128)S(1)}) custom-call(bf16[4096,1536]{1,0:T(8,128)(2,1)} %frontal.1, bf16[64,384]{1,0:T(8,128)(2,1)} %bitcast.5, s32[256]{0:T(256)} %lf_h1.1, s32[1,256]{1,0:T(1,128)} %bitcast.7, s32[1,256]{1,0:T(1,128)} %bitcast.8, s32[16,256]{1,0:T(8,128)} %bitcast.6), custom_call_target="tpu_custom_call" | custom-call | tf_op jit(solution)/shard_map/round/pallas_call | solution.py:476
  38.0 0.6 %finish.1 = (f32[64,256]{1,0:T(8,128)}, f32[16,256]{1,0:T(8,128)}, f32[1,1]{1,0:T(1,128)}) custom-call(f32[64,256]{1,0:T(8,128)S(1)} %get-tuple-element.9.a_ref, f32[16,256]{1,0:T(8,128)S(1)} %get-tuple-element.10.b_ref, f32[1,128]{1,0:T(1,128)S(1)} %get-tuple-element.11.c_ref), custom_call_target="tpu_custom_call" | custom-call | tf_op jit(solution)/shard_map/finish/pallas_call | solution.py:528

commit v4 on v3

--- a/solution.py
+++ b/solution.py
@@ -80,6 +80,7 @@
     (rows, width, p_all, ny, nx, leaves_group, skel, cap, chunk) = cfg
     n_chunk = rows // chunk
     per_run = chunk // RUN
+    half = n_chunk // 2
     tiles = rows // LANES
     half_p = p_all // 2
     sl = half_p // nx
@@ -95,6 +96,7 @@
     x = me // (2 * nx)
     q = jnp.where(core == 0, x, z)
     j_x = x * 2 + core
+    me_next = x * 2 * nx + z * 2 + 1 - core
 
     def col_of(xx, zz, cc):
         return (xx * nx + zz) * 2 + cc
@@ -149,24 +151,95 @@
 
     drains = []
 
-    def send(copy):
-        copy().start()
-        drains.append(lambda: copy().wait_send())
-
     def piece_copy(d):
         to = lax.rem(g + d, ny)
-        return remote(piece, pt.at[:, own_at], pc_send.at[d - 1], pc_recv.at[d - 1], to, me)
+        return remote(piece, pt.at[:, own_at], pc_send, pc_recv.at[d - 1], to, me)
+
+    def piece_sends():
+        at = pl.ds(0, (ny - 1) * depth)
+        remote(pt.at[:, at], pt.at[:, at], pc_send, pc_recv.at[0], g, me_next).wait_send()
 
     turns = sorted(range(1, ny), key=lambda d: min(d, ny - d))
     for d in turns:
-        send(functools.partial(piece_copy, d))
+        piece_copy(d).start()
+    drains.append(piece_sends)
 
     for d in range(1, nx):
         signal(near_sem, g, col_of(x, lax.rem(z + d, nx), core))
     for d in range(1, ny):
         signal(near_sem, lax.rem(g + d, ny), me)
 
-    for c in small:
+    for c in small[:2]:
+        c.wait()
+
+    def mask_run(t):
+        run = g * (rows // RUN) + t
+        blocks = width // RUN
+
+        @pl.when(run // blocks == me)
+        def _():
+            r0 = pl.multiple_of(t * RUN, RUN)
+            c0 = pl.multiple_of(lax.rem(run, blocks) * RUN, RUN)
+            ri = iota((RUN, RUN), 0) + run * RUN
+            ci = iota((RUN, RUN), 1) + run * RUN
+            rl = jnp.zeros((RUN, RUN), I32)
+            cl = jnp.zeros((RUN, RUN), I32)
+            for k in range(1, 4):
+                edge = lf_s[run * 4 + k]
+                rl = rl + jnp.where(ri >= edge, 1, 0)
+                cl = cl + jnp.where(ci >= edge, 1, 0)
+            block = a_v[pl.ds(r0, RUN), pl.ds(c0, RUN)].astype(F32)
+            a_v[pl.ds(r0, RUN), pl.ds(c0, RUN)] = jnp.where(rl == cl, 0.0, block).astype(jnp.bfloat16)
+
+    def product(at, d):
+        k_at = pl.ds(pl.multiple_of(lax.rem(g + d, ny) * depth, LANES), depth)
+        return dot(pt[:, k_at], a_v[at, k_at], NT)
+
+    for h in range(2):
+        for i in range(h * half, (h + 1) * half):
+            load(i).wait()
+        for t in range(h * half * per_run, (h + 1) * half * per_run):
+            mask_run(t)
+        at = pl.ds(h * half * chunk, half * chunk)
+        part[:, at] = product(at, 0)
+
+    sibling = col_of(x, z, 1 - core)
+
+    def core_copy(i):
+        at = pl.ds(pl.multiple_of(i * chunk, chunk), chunk)
+        theirs = pl.ds(pl.multiple_of((1 - core) * half_p, half_p), half_p)
+        return remote(part.at[theirs, at], cx.at[:, at], cx_send, cx_recv.at[i], g, sibling)
+
+    for d in turns[:-1]:
+        piece_copy(d).wait_recv()
+        part[...] += product(pl.ds(0, rows), ny - d)
+    piece_copy(turns[-1]).wait_recv()
+    for h in range(2):
+        at = pl.ds(h * half * chunk, half * chunk)
+        part[:, at] += product(at, ny - turns[-1])
+        for i in range(h * half, (h + 1) * half):
+            core_copy(i).start()
+    drains.append(lambda: remote(cx, cx, cx_send, cx_recv.at[0], g, sibling).wait_send())
+
+    def first_copy(i, d):
+        to = lax.rem(q + d, nx)
+        at = pl.ds(pl.multiple_of(i * chunk, chunk), chunk)
+        rows_at = pl.ds(pl.multiple_of(to * sl, sl), sl)
+        return remote(s1.at[rows_at, at], ph1.at[d - 1, :, at], p1_send, p1_recv.at[i], g, ring_a(to))
+
+    def core_sum(i, carry):
+        at = pl.ds(pl.multiple_of(i * chunk, chunk), chunk)
+        own = pl.ds(pl.multiple_of(core * half_p, half_p), half_p)
+        core_copy(i).wait_recv()
+        s1[:, at] = part[own, at] + cx[:, at]
+        for d in sorted(range(1, nx), key=lambda d: -min(d, nx - d)):
+            first_copy(i, d).start()
+        return carry
+
+    lax.fori_loop(0, n_chunk, core_sum, 0)
+    drains.append(lambda: remote(ph1, ph1, p1_send, p1_recv.at[0], g, sibling).wait_send())
+
+    for c in small[2:]:
         c.wait()
     nl = leaves_group
     lane = iota((1, LANES), 1)
@@ -229,82 +302,11 @@
     ki = LEAF_MOST * skel
     row_k = iota((ki, 1), 0) // skel
 
-    def mask_run(t):
-        run = g * (rows // RUN) + t
-        blocks = width // RUN
-
-        @pl.when(run // blocks == me)
-        def _():
-            r0 = pl.multiple_of(t * RUN, RUN)
-            c0 = pl.multiple_of(lax.rem(run, blocks) * RUN, RUN)
-            ri = iota((RUN, RUN), 0) + run * RUN
-            ci = iota((RUN, RUN), 1) + run * RUN
-            rl = jnp.zeros((RUN, RUN), I32)
-            cl = jnp.zeros((RUN, RUN), I32)
-            for k in range(1, 4):
-                edge = lf_s[run * 4 + k]
-                rl = rl + jnp.where(ri >= edge, 1, 0)
-                cl = cl + jnp.where(ci >= edge, 1, 0)
-            block = a_v[pl.ds(r0, RUN), pl.ds(c0, RUN)].astype(F32)
-            a_v[pl.ds(r0, RUN), pl.ds(c0, RUN)] = jnp.where(rl == cl, 0.0, block).astype(jnp.bfloat16)
-
-    def product(at, d):
-        k_at = pl.ds(pl.multiple_of(lax.rem(g + d, ny) * depth, LANES), depth)
-        return dot(pt[:, k_at], a_v[at, k_at], NT)
-
-    for i in range(n_chunk):
-        load(i).wait()
-        for t in range(per_run):
-            mask_run(i * per_run + t)
-        at = pl.ds(i * chunk, chunk)
-        part[:, at] = product(at, 0)
-
-    sibling = col_of(x, z, 1 - core)
-
-    def core_copy(i):
-        at = pl.ds(pl.multiple_of(i * chunk, chunk), chunk)
-        theirs = pl.ds(pl.multiple_of((1 - core) * half_p, half_p), half_p)
-        return remote(part.at[theirs, at], cx.at[:, at], cx_send.at[i], cx_recv.at[i], g, sibling)
-
-    for d in turns[:-1]:
-        piece_copy(d).wait_recv()
-        part[...] += product(pl.ds(0, rows), ny - d)
-    piece_copy(turns[-1]).wait_recv()
-    for i in range(n_chunk):
-        at = pl.ds(i * chunk, chunk)
-        part[:, at] += product(at, ny - turns[-1])
-        core_copy(i).start()
-
-    def first_copy(i, d):
-        to = lax.rem(q + d, nx)
-        at = pl.ds(pl.multiple_of(i * chunk, chunk), chunk)
-        rows_at = pl.ds(pl.multiple_of(to * sl, sl), sl)
-        s = i * (nx - 1) + d - 1
-        return remote(s1.at[rows_at, at], ph1.at[d - 1, :, at], p1_send.at[s], p1_recv.at[s], g, ring_a(to))
-
-    def core_sum(i, carry):
-        at = pl.ds(pl.multiple_of(i * chunk, chunk), chunk)
-        own = pl.ds(pl.multiple_of(core * half_p, half_p), half_p)
-        core_copy(i).wait_recv()
-        s1[:, at] = part[own, at] + cx[:, at]
-        for d in range(1, nx):
-            first_copy(i, d).start()
-        return carry
-
-    def drain(i, carry):
-        core_copy(i).wait_send()
-        for d in range(1, nx):
-            first_copy(i, d).wait_send()
-        return carry
-
-    lax.fori_loop(0, n_chunk, core_sum, 0)
-    drains.append(lambda: lax.fori_loop(0, n_chunk, drain, 0))
-
     rot[per_tile * tiles] = jnp.zeros((sl, LANES), F32)
 
     def first_sum(i, carry):
-        for d in range(1, nx):
-            first_copy(i, d).wait_recv()
+        every = ph1.at[:, :, pl.ds(pl.multiple_of(i * chunk, chunk), chunk)]
+        remote(every, every, p1_send, p1_recv.at[i], g, sibling).wait_recv()
         own = pl.ds(pl.multiple_of(q * sl, sl), sl)
         for t in range(chunk // LANES):
             at = pl.ds(pl.multiple_of(i * chunk + t * LANES, LANES), LANES)
@@ -328,11 +330,7 @@
         return col_of(lax.rem(x + dx, nx), lax.rem(z + dz, nx), lax.rem(core + dc, 2))
 
     def owner_copy(n, k):
-        return remote(pk.at[n], rx.at[me], o_send.at[n], o_recv.at[me], g, there(k))
-
-    def owner_wait(n, k):
-        frm = there(k)
-        return remote(pk.at[n], rx.at[frm], o_send.at[n], o_recv.at[frm], g, frm)
+        return remote(pk.at[n], rx.at[me], o_send, o_recv, g, there(k))
 
     def block_of(o, h):
         base = o * per_owner + h * per_tile
@@ -348,11 +346,12 @@
         o = there(k)
         for h in range(cap // LANES):
             pk[n, :, h * LANES : (h + 1) * LANES] = block_of(o, h)
-        send(functools.partial(owner_copy, n, k))
+        owner_copy(n, k).start()
     for h in range(cap // LANES):
         rx[me, :, h * LANES : (h + 1) * LANES] = block_of(me, h)
-    for n, k in reversed(list(enumerate(steps))):
-        owner_wait(n, k).wait_recv()
+    blocks_in = remote(pk, rx.at[: n_col - 1], o_send, o_recv, g, sibling)
+    blocks_in.wait_recv()
+    drains.append(blocks_in.wait_send)
 
     def total(ids):
         v = rx[ids[0]]
@@ -414,32 +413,33 @@
     def m1(d):
         j = lax.rem(j_x + d, owners)
         to = col_of(j // 2, z, lax.rem(j, 2))
-        return remote(w0.at[:1], w1.at[d - 1, :1], m_send.at[d - 1], m_recv.at[d - 1], g, to)
+        return remote(w0.at[:1], w1.at[d - 1, :1], m_send.at[0], m_recv.at[0], g, to)
 
     def m2(d):
-        s = owners - 2 + d
         to_y = lax.rem(g + d // nx, ny)
         to = col_of(x, lax.rem(z + d % nx, nx), core)
-        return remote(w2.at[:1], w3.at[d - 1, :1], m_send.at[s], m_recv.at[s], to_y, to)
-
-    for d in range(1, owners):
-        send(functools.partial(m1, d))
+        return remote(w2.at[:1], w3.at[d - 1, :1], m_send.at[1], m_recv.at[1], to_y, to)
+
+    for d in sorted(range(1, owners), key=lambda d: -min(d, owners - d)):
+        m1(d).start()
     folded_c = coeff[:skel]
     for k in range(1, LEAF_MOST):
         folded_c = folded_c + coeff[k * skel : (k + 1) * skel]
     interp_out[...] = folded_c
-    for d in range(1, owners):
-        m1(d).wait_recv()
+    all1 = remote(w1.at[:, :1], w1.at[:, :1], m_send.at[0], m_recv.at[0], g, sibling)
+    all1.wait_recv()
     v = w0[:1]
     for d in range(1, owners):
         v = jnp.maximum(v, w1[d - 1, :1])
     w2[...] = jnp.broadcast_to(v, w2.shape)
-    for d in range(1, nx * ny):
-        send(functools.partial(m2, d))
+    for d in sorted(range(1, nx * ny), key=lambda d: -min(d % nx, nx - d % nx) - min(d // nx, ny - d // nx)):
+        m2(d).start()
     for f in drains:
         f()
-    for d in range(1, nx * ny):
-        m2(d).wait_recv()
+    all1.wait_send()
+    all2 = remote(w3.at[:, :1], w3.at[:, :1], m_send.at[1], m_recv.at[1], g, sibling)
+    all2.wait_send()
+    all2.wait_recv()
     for d in range(1, nx * ny):
         v = jnp.maximum(v, w3[d - 1, :1])
     worst_out[...] = v
@@ -470,7 +470,6 @@
     hbm = pl.BlockSpec(memory_space=pl.ANY)
     vmem = pl.BlockSpec(memory_space=pltpu.VMEM)
     dma = pltpu.SemaphoreType.DMA
-    n_m = owners - 1 + nx * ny - 1
     pad = ((0, 0), (0, max(0, LANES - leaves)))
     wide = leaves + pad[1][1]
     results = pl.pallas_call(
@@ -502,16 +501,16 @@
             dma((5,)),
             dma(()),
             pltpu.SemaphoreType.REGULAR,
+            dma(()),
             dma((ny - 1,)),
-            dma((ny - 1,)),
+            dma(()),
             dma((n_chunk,)),
+            dma(()),
             dma((n_chunk,)),
-            dma((n_chunk * (nx - 1),)),
-            dma((n_chunk * (nx - 1),)),
-            dma((n_col,)),
-            dma((n_col,)),
-            dma((n_m,)),
-            dma((n_m,)),
+            dma(()),
+            dma(()),
+            dma((2,)),
+            dma((2,)),
         ],
         compiler_params=pltpu.CompilerParams(
             collective_id=0, has_side_effects=True, vmem_limit_bytes=56 << 20

time: 38.8 us -> 36.7 us (0.946)
  Pallas kernels: 38.1 us -> 36 us
    pallas_call x1, Pallas kernels: 37.4 us -> 35.3 us  [local(): pl.pallas_call(functools.partial(kernel, cfg), out_shape=out_kind((p_all,...]
where the time goes in v4:
time: 36.7 us; the launch traced here: 36.6 us
  Pallas kernels  36 us (98%)
  between operations  0.64 us (2%)
    pallas_call x1, Pallas kernels, local(): pl.pallas_call(functools.partial(kernel, cfg), out_shape=out_kind((p_all,...  35.3 us

profile of v4, /device:TPU:0, one launch (start us, length us, event | category | flops | bytes accessed | tf_op | source)
XLA Modules:
  0.0 36.6 jit_solution(9835156271399194772)
XLA Ops:
  0.6 35.3 %round.1 = (f32[64,256]{1,0:T(8,128)S(1)}, f32[16,256]{1,0:T(8,128)S(1)}, f32[1,128]{1,0:T(1,128)S(1)}) custom-call(bf16[4096,1536]{1,0:T(8,128)(2,1)} %frontal.1, bf16[64,384]{1,0:T(8,128)(2,1)} %bitcast.5, s32[256]{0:T(256)} %lf_h1.1, s32[1,256]{1,0:T(1,128)} %bitcast.7, s32[1,256]{1,0:T(1,128)} %bitcast.8, s32[16,256]{1,0:T(8,128)} %bitcast.6), custom_call_target="tpu_custom_call" | custom-call | tf_op jit(solution)/shard_map/round/pallas_call | solution.py:475
  36.0 0.6 %finish.1 = (f32[64,256]{1,0:T(8,128)}, f32[16,256]{1,0:T(8,128)}, f32[1,1]{1,0:T(1,128)}) custom-call(f32[64,256]{1,0:T(8,128)S(1)} %get-tuple-element.9.a_ref, f32[16,256]{1,0:T(8,128)S(1)} %get-tuple-element.10.b_ref, f32[1,128]{1,0:T(1,128)S(1)} %get-tuple-element.11.c_ref), custom_call_target="tpu_custom_call" | custom-call | tf_op jit(solution)/shard_map/finish/pallas_call | solution.py:527

commit v5 on v4

--- a/solution.py
+++ b/solution.py
@@ -147,13 +147,14 @@
         c.start()
     for i in range(n_chunk):
         load(i).start()
+    small[0].wait()
     pl.semaphore_wait(barrier, count)
 
     drains = []
 
     def piece_copy(d):
         to = lax.rem(g + d, ny)
-        return remote(piece, pt.at[:, own_at], pc_send, pc_recv.at[d - 1], to, me)
+        return remote(pt.at[:, own_at], pt.at[:, own_at], pc_send, pc_recv.at[d - 1], to, me)
 
     def piece_sends():
         at = pl.ds(0, (ny - 1) * depth)
@@ -169,8 +170,7 @@
     for d in range(1, ny):
         signal(near_sem, lax.rem(g + d, ny), me)
 
-    for c in small[:2]:
-        c.wait()
+    small[1].wait()
 
     def mask_run(t):
         run = g * (rows // RUN) + t
@@ -210,33 +210,36 @@
         theirs = pl.ds(pl.multiple_of((1 - core) * half_p, half_p), half_p)
         return remote(part.at[theirs, at], cx.at[:, at], cx_send, cx_recv.at[i], g, sibling)
 
-    for d in turns[:-1]:
-        piece_copy(d).wait_recv()
-        part[...] += product(pl.ds(0, rows), ny - d)
-    piece_copy(turns[-1]).wait_recv()
-    for h in range(2):
-        at = pl.ds(h * half * chunk, half * chunk)
-        part[:, at] += product(at, ny - turns[-1])
-        for i in range(h * half, (h + 1) * half):
-            core_copy(i).start()
-    drains.append(lambda: remote(cx, cx, cx_send, cx_recv.at[0], g, sibling).wait_send())
-
     def first_copy(i, d):
         to = lax.rem(q + d, nx)
         at = pl.ds(pl.multiple_of(i * chunk, chunk), chunk)
         rows_at = pl.ds(pl.multiple_of(to * sl, sl), sl)
         return remote(s1.at[rows_at, at], ph1.at[d - 1, :, at], p1_send, p1_recv.at[i], g, ring_a(to))
 
-    def core_sum(i, carry):
+    def core_sum(i):
         at = pl.ds(pl.multiple_of(i * chunk, chunk), chunk)
         own = pl.ds(pl.multiple_of(core * half_p, half_p), half_p)
         core_copy(i).wait_recv()
         s1[:, at] = part[own, at] + cx[:, at]
         for d in sorted(range(1, nx), key=lambda d: -min(d, nx - d)):
             first_copy(i, d).start()
-        return carry
-
-    lax.fori_loop(0, n_chunk, core_sum, 0)
+
+    piece_copy(turns[0]).wait_recv()
+    part[...] += product(pl.ds(0, rows), ny - turns[0])
+    for d in turns[1:]:
+        piece_copy(d).wait_recv()
+    lag = 2
+    for i in range(n_chunk + lag):
+        if i < n_chunk:
+            at = pl.ds(i * chunk, chunk)
+            v = part[:, at]
+            for d in turns[1:]:
+                v = v + product(at, ny - d)
+            part[:, at] = v
+            core_copy(i).start()
+        if i >= lag:
+            core_sum(i - lag)
+    drains.append(lambda: remote(cx, cx, cx_send, cx_recv.at[0], g, sibling).wait_send())
     drains.append(lambda: remote(ph1, ph1, p1_send, p1_recv.at[0], g, sibling).wait_send())
 
     for c in small[2:]:
@@ -459,7 +462,7 @@
     ny = lax.axis_size("row")
     nx = math.isqrt(n_col // 2)
     cap = 2 * rows // n_col
-    chunk = 512
+    chunk = rows // 4
     n_chunk = rows // chunk
     tiles = rows // LANES
     half_p = p_all // 2

time: 36.7 us -> 35.7 us (0.973)
  Pallas kernels: 36 us -> 34.9 us
    pallas_call x1, Pallas kernels: 35.3 us -> 34.3 us  [local(): pl.pallas_call(functools.partial(kernel, cfg), out_shape=out_kind((p_all,...]
where the time goes in v5:
time: 35.7 us; the launch traced here: 35.5 us
  Pallas kernels  34.9 us (98%)
  between operations  0.64 us (2%)
    pallas_call x1, Pallas kernels, local(): pl.pallas_call(functools.partial(kernel, cfg), out_shape=out_kind((p_all,...  34.3 us

profile of v5, /device:TPU:0, one launch (start us, length us, event | category | flops | bytes accessed | tf_op | source)
XLA Modules:
  0.0 35.5 jit_solution(13218622439281075697)
XLA Ops:
  0.6 34.3 %round.1 = (f32[64,256]{1,0:T(8,128)S(1)}, f32[16,256]{1,0:T(8,128)S(1)}, f32[1,128]{1,0:T(1,128)S(1)}) custom-call(bf16[4096,1536]{1,0:T(8,128)(2,1)} %frontal.1, bf16[64,384]{1,0:T(8,128)(2,1)} %bitcast.5, s32[256]{0:T(256)} %lf_h1.1, s32[1,256]{1,0:T(1,128)} %bitcast.7, s32[1,256]{1,0:T(1,128)} %bitcast.8, s32[16,256]{1,0:T(8,128)} %bitcast.6), custom_call_target="tpu_custom_call" | custom-call | tf_op jit(solution)/shard_map/round/pallas_call | solution.py:478
  34.9 0.6 %finish.1 = (f32[64,256]{1,0:T(8,128)}, f32[16,256]{1,0:T(8,128)}, f32[1,1]{1,0:T(1,128)}) custom-call(f32[64,256]{1,0:T(8,128)S(1)} %get-tuple-element.9.a_ref, f32[16,256]{1,0:T(8,128)S(1)} %get-tuple-element.10.b_ref, f32[1,128]{1,0:T(1,128)S(1)} %get-tuple-element.11.c_ref), custom_call_target="tpu_custom_call" | custom-call | tf_op jit(solution)/shard_map/finish/pallas_call | solution.py:530

commit v6 on v5

--- a/solution.py
+++ b/solution.py
@@ -343,7 +343,15 @@
         return v
 
     steps = [(dx, dz, dc) for dx in range(nx) for dz in range(nx) for dc in range(2)]
-    steps.sort(key=lambda k: -(min(k[0], nx - k[0]) + min(k[1], nx - k[1])))
+    turn_of = {n: m for m, n in enumerate([1, nx - 1, *range(2, nx - 1), 0])}
+    steps.sort(
+        key=lambda k: (
+            -(min(k[0], nx - k[0]) + min(k[1], nx - k[1])),
+            k[2],
+            turn_of[k[1]],
+            turn_of[k[0]],
+        )
+    )
     steps = [k for k in steps if k != (0, 0, 0)]
     for n, k in enumerate(steps):
         o = there(k)
@@ -369,8 +377,14 @@
     )
 
     samples_out[...] = m
-    pick = dot(hot, m, NT, HI)
-    pick_t = dot(m, hot, NT, HI)
+    terms = []
+    rest = m
+    for _ in range(3):
+        terms.append(rest.astype(jnp.bfloat16))
+        rest = rest - terms[-1].astype(F32)
+    hot16 = hot.astype(jnp.bfloat16)
+    pick = sum(dot(hot16, t, NT) for t in terms)
+    pick_t = sum(dot(t, hot16, NT) for t in terms)
     rhs = dot(pick, m, NN, HI)
     gram = dot(pick, pick, NT, HI)
     col_k = iota((1, ki), 1) // skel

time: 35.7 us -> 35.5 us (level)
  no operation moved by 1% of the time
where the time goes in v6:
time: 35.5 us; the launch traced here: 35.3 us
  Pallas kernels  34.7 us (98%)
  between operations  0.64 us (2%)
    pallas_call x1, Pallas kernels, local(): pl.pallas_call(functools.partial(kernel, cfg), out_shape=out_kind((p_all,...  34.1 us

profile of v6, /device:TPU:0, one launch (start us, length us, event | category | flops | bytes accessed | tf_op | source)
XLA Modules:
  0.0 35.3 jit_solution(987028397336150855)
XLA Ops:
  0.6 34.1 %round.1 = (f32[64,256]{1,0:T(8,128)S(1)}, f32[16,256]{1,0:T(8,128)S(1)}, f32[1,128]{1,0:T(1,128)S(1)}) custom-call(bf16[4096,1536]{1,0:T(8,128)(2,1)} %frontal.1, bf16[64,384]{1,0:T(8,128)(2,1)} %bitcast.5, s32[256]{0:T(256)} %lf_h1.1, s32[1,256]{1,0:T(1,128)} %bitcast.7, s32[1,256]{1,0:T(1,128)} %bitcast.8, s32[16,256]{1,0:T(8,128)} %bitcast.6), custom_call_target="tpu_custom_call" | custom-call | tf_op jit(solution)/shard_map/round/pallas_call | solution.py:492
  34.7 0.6 %finish.1 = (f32[64,256]{1,0:T(8,128)}, f32[16,256]{1,0:T(8,128)}, f32[1,1]{1,0:T(1,128)}) custom-call(f32[64,256]{1,0:T(8,128)S(1)} %get-tuple-element.9.a_ref, f32[16,256]{1,0:T(8,128)S(1)} %get-tuple-element.10.b_ref, f32[1,128]{1,0:T(1,128)S(1)} %get-tuple-element.11.c_ref), custom_call_target="tpu_custom_call" | custom-call | tf_op jit(solution)/shard_map/finish/pallas_call | solution.py:544
